TPU v7x, 512 devices: a whole 4x8x8 slice. The times are simulated.
512 devices in a mesh: outer: 16 (over y, core), inner: 32 (over x, z).
Axes of the slice: x: 4, y: 8, z: 8, core: 2. Of those that a mesh axis runs over, the one named last changes fastest.
Arguments:
- queries: bfloat16 [32768, 4096], P('inner', 'outer'), may hold values from -150 to 150
- keys: bfloat16 [32768, 4096], P('inner', 'outer'), may hold values from -7 to 7
- values: bfloat16 [32768, 4096], P('inner', 'outer'), may hold values from -18 to 18
- counts: int32 [256], P('inner'), may hold values from 1 to 128, 24576 in all
- window_mask: int32 [256, 3], P('inner'), may hold values 0 or 1
- norm_gain: float32 [4096], P('outer'), may hold values from 0.5 to 1.5
Outputs:
- attended: bfloat16 [32768, 4096], P('inner', 'outer')
Inputs may be any that keep to these rules, and one draw needn't show every extreme that they name: `counts`: the largest count is exactly 128.
All inputs are finite; a program needn't handle non-finite values. No bound on the sum of `counts` or of `window_mask` on one device may be relied on, other than what follows from the above.
Results may differ from a plain program's by a relative error of at most 0.0048.
Values may be sent and summed in bfloat16 or wider, within the bound.
A program may use at most 64 MiB of HBM per device.

v0:
```python
import jax
import jax.numpy as jnp
from jax import lax
from jax.sharding import PartitionSpec as P

HD = 128
BLK = 128
PREV = 3
WIDTH = 4096


def carried_in(part, axis, combine, identity):
    place = lax.axis_index(axis)
    gathered = lax.all_gather(part, axis)
    state = jnp.zeros_like(part) + jnp.asarray(identity, part.dtype)

    def one(step, state):
        return combine(state, lax.dynamic_index_in_dim(gathered, step, 0, False))

    return lax.fori_loop(0, place, one, state)


def from_behind(value, axis, steps):
    count = lax.axis_size(axis)
    first, last = (max(0, -steps), min(count, count - steps))
    return lax.ppermute(value, axis, [(source, source + steps) for source in range(first, last)])


def add_states(earlier, later):
    return earlier + later


def shards(queries, keys, values, counts, window_mask, norm_gain):
    tok_rows = queries.shape[0]
    groups_here = tok_rows // BLK
    local_heads = queries.shape[1] // HD
    position = lax.broadcasted_iota(jnp.int32, (BLK,), 0)
    key_valid = position[None, :] < counts[:, None]
    masked_keys = jnp.where(key_valid.reshape(tok_rows)[:, None], keys, jnp.zeros((), jnp.bfloat16))
    query_blocks = queries.reshape(groups_here, BLK, local_heads, HD)
    key_blocks = masked_keys.reshape(groups_here, BLK, local_heads, HD)
    value_blocks = values.reshape(groups_here, BLK, local_heads, HD)
    group_states = jnp.einsum(
        "cshd,cshe->chde", key_blocks, value_blocks, preferred_element_type=jnp.float32
    )
    running = jnp.cumsum(group_states, axis=0)
    within = jnp.concatenate([jnp.zeros_like(group_states[:1]), running[:-1]], axis=0)
    span_total = running[-1]
    before = carried_in(span_total, "inner", add_states, jnp.zeros_like(span_total))
    prior_rounded = (before[None] + within).astype(jnp.bfloat16)
    rim_rows = PREV * BLK
    rim_keys, rim_values, rim_counts = from_behind(
        (
            masked_keys[tok_rows - rim_rows :],
            values[tok_rows - rim_rows :],
            counts[groups_here - PREV :],
        ),
        "inner",
        1,
    )
    extended_keys = jnp.concatenate([rim_keys, masked_keys], axis=0).reshape(
        groups_here + PREV, BLK, local_heads, HD
    )
    extended_values = jnp.concatenate([rim_values, values], axis=0).reshape(
        groups_here + PREV, BLK, local_heads, HD
    )
    extended_counts = jnp.concatenate([rim_counts, counts], axis=0)
    extended_valid = position[None, :] < extended_counts[:, None]
    window_keys = jnp.stack(
        [extended_keys[place : place + groups_here] for place in range(PREV + 1)], axis=1
    ).reshape(groups_here, (PREV + 1) * BLK, local_heads, HD)
    window_values = jnp.stack(
        [extended_values[place : place + groups_here] for place in range(PREV + 1)], axis=1
    ).reshape(groups_here, (PREV + 1) * BLK, local_heads, HD)
    window_valid = jnp.stack(
        [extended_valid[place : place + groups_here] for place in range(PREV + 1)], axis=1
    )
    group_on = jnp.concatenate(
        [window_mask[:, ::-1] == 1, jnp.ones((groups_here, 1), jnp.bool_)], axis=1
    )
    causal = position[:, None] >= position[None, :]
    causal_full = jnp.concatenate([jnp.ones((BLK, PREV * BLK), jnp.bool_), causal], axis=1)
    allowed = (window_valid & group_on[:, :, None]).reshape(
        groups_here, 1, (PREV + 1) * BLK
    ) & causal_full[None]
    score_scale = 1.0 / HD**0.5
    scores = (
        jnp.einsum("cthd,cshd->chts", query_blocks, window_keys, preferred_element_type=jnp.float32)
        * score_scale
    )
    scores = jnp.where(allowed[:, None], scores, -1e30)
    largest = jnp.max(scores, axis=-1, keepdims=True)
    expd = jnp.exp(scores - largest)
    weights = (expd / jnp.sum(expd, axis=-1, keepdims=True)).astype(jnp.bfloat16)
    local_part = jnp.einsum(
        "chts,cshd->cthd", weights, window_values, preferred_element_type=jnp.float32
    )
    inter = jnp.einsum(
        "cthd,chde->cthe", query_blocks, prior_rounded, preferred_element_type=jnp.float32
    )
    intra_weights = jnp.einsum(
        "cthd,cshd->chts", query_blocks, key_blocks, preferred_element_type=jnp.float32
    )
    intra_weights = jnp.where(causal[None, None], intra_weights, 0.0).astype(jnp.bfloat16)
    intra = jnp.einsum(
        "chts,cshe->cthe", intra_weights, value_blocks, preferred_element_type=jnp.float32
    )
    linear_part = inter + intra
    local_squares = jnp.sum(linear_part * linear_part, axis=(2, 3))
    row_squares = lax.psum(local_squares, "outer")
    normed = linear_part * lax.rsqrt(row_squares / WIDTH + 1e-06)[:, :, None, None]
    result = normed * norm_gain.reshape(local_heads, HD)[None, None] + local_part
    return result.reshape(tok_rows, local_heads * HD).astype(jnp.bfloat16)


def solution(mesh):
    return jax.shard_map(
        shards,
        mesh=mesh,
        in_specs=(
            P("inner", "outer"),
            P("inner", "outer"),
            P("inner", "outer"),
            P("inner"),
            P("inner", None),
            P("outer"),
        ),
        out_specs=P("inner", "outer"),
        check_vma=False,
    )
```

profile of v0, /device:TPU:7, one launch (start us, length us, event | category | flops | bytes accessed | tf_op | source)
XLA Modules:
  0.0 166.0 jit_solution(16054141134522092386)
XLA Ops:
  7.3 1.2 broadcast_select_fusion
  8.7 1.2 reshape.85
  13.4 4.0 %collective-permute-start.2 = (bf16[384,256]{1,0:T(8,128)(2,1)}, bf16[384,256]{1,0:T(8,128)(2,1)S(1)}, u32[]{:S(2)}, u32[]{:S(2)}) collective-permute-start(bf16[384,256]{1,0:T(8,128)(2,1)} %slice.79), channel_id=1, source_target_pairs={{0,1},{1,2},{2,3},{3,4},{4,5},{5,6},{6,7},{7,8},{8,9},{9,10},{10,1... | collective-permute-start | bytes 589832 | tf_op jit(solution)/shard_map/ppermute | solution.py:26
  18.1 4.0 %collective-permute-start.1 = (s32[3]{0:T(128)}, s32[3]{0:T(128)}, u32[]{:S(2)}, u32[]{:S(2)}) collective-permute-start(s32[3]{0:T(128)} %slice.61), channel_id=1, source_target_pairs={{0,1},{1,2},{2,3},{3,4},{4,5},{5,6},{6,7},{7,8},{8,9},{9,10},{10,1... | collective-permute-start | bytes 44 | tf_op jit(solution)/shard_map/ppermute | solution.py:26
  22.8 4.0 %collective-permute-start = (bf16[384,256]{1,0:T(8,128)(2,1)}, bf16[384,256]{1,0:T(8,128)(2,1)S(1)}, u32[]{:S(2)}, u32[]{:S(2)}) collective-permute-start(bf16[384,256]{1,0:T(8,128)(2,1)} %slice.57), channel_id=1, source_target_pairs={{0,1},{1,2},{2,3},{3,4},{4,5},{5,6},{6,7},{7,8},{8,9},{9,10},{10,1... | collective-permute-start | bytes 589832 | tf_op jit(solution)/shard_map/ppermute | solution.py:26
  28.6 2.0 %copy.56 = bf16[8,1,128,2,128]{4,2,1,3,0:T(8,128)(2,1)} copy(bf16[8,1,128,2,128]{4,3,2,0,1:T(2,128)(2,1)} %stack.58) | data formatting | bytes 1048576 | tf_op jit(solution)/shard_map/stack | solution.py:69
  31.9 3.8 %copy.52 = bf16[8,1,128,2,128]{2,1,4,3,0:T(2,128)(2,1)} copy(bf16[8,1,128,2,128]{4,3,2,0,1:T(2,128)(2,1)} %stack.48) | data formatting | bytes 1048576 | tf_op jit(solution)/shard_map/stack | solution.py:72
  36.6 1.4 broadcast_and_fusion
  38.9 1.2 stack.55
  44.2 1.2 stack.45
  45.4 2.0 %copy.49 = bf16[8,1,128,2,128]{2,1,4,3,0:T(2,128)(2,1)} copy(bf16[8,1,128,2,128]{4,3,2,0,1:T(2,128)(2,1)S(1)} %stack.45) | data formatting | bytes 1048576 | tf_op jit(solution)/shard_map/stack | solution.py:72
  47.4 1.2 stack.46
  48.6 2.0 %copy.50 = bf16[8,1,128,2,128]{2,1,4,3,0:T(2,128)(2,1)} copy(bf16[8,1,128,2,128]{4,3,2,0,1:T(2,128)(2,1)S(1)} %stack.46) | data formatting | bytes 1048576 | tf_op jit(solution)/shard_map/stack | solution.py:72
  50.7 2.0 %copy.51 = bf16[8,1,128,2,128]{2,1,4,3,0:T(2,128)(2,1)} copy(bf16[8,1,128,2,128]{4,3,2,0,1:T(2,128)(2,1)S(1)} %stack.47) | data formatting | bytes 1048576 | tf_op jit(solution)/shard_map/stack | solution.py:72
  52.7 6.4 %pad_maximum_fusion = bf16[8,4,128,2,128]{2,1,4,3,0:T(4,128)(2,1)S(1)} fusion(bf16[8,1,128,2,128]{2,1,4,3,0:T(2,128)(2,1)} %copy.52, bf16[8,1,128,2,128]{2,1,4,3,0:T(2,128)(2,1)} %copy.51, bf16[8,1,128,2,128]{2,1,4,3,0:T(2,128)(2,1)} %copy.50, bf16[8,1,128,2,128]{2,1,4,3,0:T(2,128)(2,1)} %copy.49), kind=kLoop, calls=%fused_computation.6 | loop fusion | flops 8388608 | bytes 4194304 | tf_op jit(solution)/shard_map/stack | solution.py:72
  59.1 2.2 %reshape.87 = bf16[8,512,2,128]{1,3,2,0:T(8,128)(2,1)} reshape(bf16[8,4,128,2,128]{2,1,4,3,0:T(4,128)(2,1)S(1)} %pad_maximum_fusion) | data formatting | bytes 4194304 | tf_op jit(solution)/shard_map/reshape | solution.py:74
  61.3 1.8 %pad_maximum_fusion.1 = bf16[8,4,128,2,128]{4,2,1,3,0:T(8,128)(2,1)S(1)} fusion(bf16[8,1,128,2,128]{4,2,1,3,0:T(8,128)(2,1)} %copy.56, bf16[8,1,128,2,128]{4,2,1,3,0:T(8,128)(2,1)} %copy.55, bf16[8,1,128,2,128]{4,2,1,3,0:T(8,128)(2,1)} %copy.54, bf16[8,1,128,2,128]{4,2,1,3,0:T(8,128)(2,1)} %copy.53), kind=kLoop, calls=%fused_computation.7 | loop fusion | flops 3145728 | bytes 4194304 | tf_op jit(solution)/shard_map/stack | solution.py:69
  64.2 3.9 %fusion.33 = (f32[8,2,128]{2,1,0:T(2,128)S(1)}, f32[8,2,128,512]{2,3,1,0:T(8,128)}) fusion(f32[8,2,512,128]{3,2,1,0:T(8,128)S(1)} %fusion.21, pred[8,128,512]{1,2,0:T(8,128)(4,1)S(1)} %copy-done.4), kind=kOutput, calls=%fused_computation.63 | output fusion | flops 6291967 | bytes 8921088 | tf_op jit(solution)/shard_map/sub | solution.py:93
  68.0 32.9 %all-gather.2.cloned.1.call-done = f32[32,2,128,128]{3,2,1,0:T(8,128)} async-done(((f32[1,2,128,128]{3,2,1,0:T(8,128)}), f32[32,2,128,128]{3,2,1,0:T(8,128)}) %all-gather.2.cloned.1.call-update) | async-done | bytes 4194320 | tf_op jit(solution)/shard_map/all_gather | solution.py:14
  100.9 23.1 %while.10 = (s32[]{:T(128)}, f32[2,128,128]{2,1,0:T(8,128)S(1)}, s32[]{:T(128)}, f32[32,2,128,128]{3,2,1,0:T(8,128)}, s32[]{:T(128)}, /*index=5*/s32[]{:T(128)}, s32[]{:T(128)}) while((s32[]{:T(128)}, f32[2,128,128]{2,1,0:T(8,128)S(1)}, s32[]{:T(128)}, f32[32,2,128,128]{3,2,1,0:T(8,128)}, s32[]{:T(128)}, /*index=5*/s32[]{:T(128)}, ...), condition=%wide.region_2.3_spmd, body=%wide.region_1.2_spmd.sunk | while | flops 32773 | bytes 393331 | solution.py:20
  124.1 1.5 convolution_bitcast_fusion.2
  125.6 1.9 %multiply_reduce_fusion = (f32[8,128]{1,0:T(8,128)S(1)}, f32[8,128,2,128]{1,3,2,0:T(8,128)S(1)}) fusion(f32[8,128,2,128]{1,3,2,0:T(8,128)} %convolution_bitcast_fusion.2, bf16[8,128,2,128]{1,3,2,0:T(8,128)(2,1)S(1)} %copy-done.2, pred[128,128]{0,1:T(8,128)(4,1)S(1)} %iota_compare_fusion, bf16[8,128,2,128]{3,2,1,0:T(2,128)(2,1)S(1)} %reshape.84, ...), kind=kOutput, calls=%fused_computation.21 | convolution fusion | flops 135527424 | bytes 3690496 | tf_op jit(solution)/shard_map/chts,cshe->cthe/dot_general | solution.py:105
  127.5 26.7 %psum.7 = f32[8,128]{1,0:T(8,128)S(1)} all-reduce(f32[8,128]{1,0:T(8,128)S(1)} %get-tuple-element.49), channel_id=1, replica_groups=mesh['outer'=16,'inner'=32] {'outer'}, use_global_device_ids=true, to_apply=%region_4.5 | all-reduce | flops 1024 | bytes 8192 | tf_op jit(solution)/shard_map/psum | solution.py:110
  154.2 3.5 %fusion.10 = bf16[8,128,2,128]{1,3,2,0:T(8,128)(2,1)S(1)} fusion(bf16[8,512,2,128]{1,3,2,0:T(8,128)(2,1)} %reshape.87, f32[8,2,128,512]{2,3,1,0:T(8,128)} %get-tuple-element.48, f32[8,2,128]{2,1,0:T(2,128)S(1)} %get-tuple-element.47, f32[8,128,2,128]{1,3,2,0:T(8,128)S(1)} %get-tuple-element.50, f32[2,128]{1,0:T(2,128)S(1)} %bitcast.65, ...), kind=kOutput, calls=%fused_computation.19 | convolution fusion | flops 271581184 | bytes 7877632 | tf_op jit(solution)/shard_map/chts,cshd->cthd/dot_general | solution.py:95
  (83 shorter events, 39.7 us)
Async XLA Ops:
  6.5 94.4 %all-gather.2.cloned.1.call-start = ((), (), s32[]{:S(2)}) async-start(), calls=%async_computation | async-start | bytes 4325376 | tf_op jit(solution)/shard_map/all_gather | solution.py:14
  8.5 8.9 %copy-start.7 = (s32[8]{0:T(128)S(1)}, s32[8]{0:T(128)}, u32[]{:S(2)}) copy-start(s32[8]{0:T(128)} %param.11) | copy-start | bytes 100
  8.5 13.5 %copy-start = (bf16[1024,256]{1,0:T(8,128)(2,1)S(1)}, bf16[1024,256]{1,0:T(8,128)(2,1)}, u32[]{:S(2)}) copy-start(bf16[1024,256]{1,0:T(8,128)(2,1)} %param.10) | copy-start | bytes 1572868
  10.3 18.3 %copy-start.1 = (bf16[8,128,2,128]{1,3,2,0:T(8,128)(2,1)}, bf16[8,128,2,128]{1,3,2,0:T(8,128)(2,1)S(1)}, u32[]{:S(2)}) copy-start(bf16[8,128,2,128]{1,3,2,0:T(8,128)(2,1)S(1)} %copy.48) | copy-start | bytes 1572868
  10.8 20.9 %copy-start.5 = (s32[8,3]{0,1:T(4,128)S(1)}, s32[8,3]{0,1:T(4,128)}, u32[]{:S(2)}) copy-start(s32[8,3]{0,1:T(4,128)} %param.12) | copy-start | bytes 292
  11.9 16.6 %copy-start.3 = (f32[8,2,128,128]{3,2,1,0:T(8,128)}, f32[8,2,128,128]{3,2,1,0:T(8,128)S(1)}, u32[]{:S(2)}) copy-start(f32[8,2,128,128]{3,2,1,0:T(8,128)S(1)} %fusion.38) | copy-start | bytes 3145732
  13.4 24.6 %collective-permute-start.2 = (bf16[384,256]{1,0:T(8,128)(2,1)}, bf16[384,256]{1,0:T(8,128)(2,1)S(1)}, u32[]{:S(2)}, u32[]{:S(2)}) collective-permute-start(bf16[384,256]{1,0:T(8,128)(2,1)} %slice.79), channel_id=1, source_target_pairs={{0,1},{1,2},{2,3},{3,4},{4,5},{5,6},{6,7},{7,8},{8,9},{9,10},{10,1... | collective-permute-start | bytes 589832 | tf_op jit(solution)/shard_map/ppermute | solution.py:26
  18.1 17.6 %collective-permute-start.1 = (s32[3]{0:T(128)}, s32[3]{0:T(128)}, u32[]{:S(2)}, u32[]{:S(2)}) collective-permute-start(s32[3]{0:T(128)} %slice.61), channel_id=1, source_target_pairs={{0,1},{1,2},{2,3},{3,4},{4,5},{5,6},{6,7},{7,8},{8,9},{9,10},{10,1... | collective-permute-start | bytes 44 | tf_op jit(solution)/shard_map/ppermute | solution.py:26
  22.8 20.3 %collective-permute-start = (bf16[384,256]{1,0:T(8,128)(2,1)}, bf16[384,256]{1,0:T(8,128)(2,1)S(1)}, u32[]{:S(2)}, u32[]{:S(2)}) collective-permute-start(bf16[384,256]{1,0:T(8,128)(2,1)} %slice.57), channel_id=1, source_target_pairs={{0,1},{1,2},{2,3},{3,4},{4,5},{5,6},{6,7},{7,8},{8,9},{9,10},{10,1... | collective-permute-start | bytes 589832 | tf_op jit(solution)/shard_map/ppermute | solution.py:26
  63.1 1.0 copy-start.4
  64.2 59.9 %slice-start = ((f32[8,2,128,128]{3,2,1,0:T(8,128)}), f32[7,2,128,128]{3,2,1,0:T(8,128)S(1)}, s32[]{:S(2)}) async-start(f32[8,2,128,128]{3,2,1,0:T(8,128)} %copy-done.3), calls=%async_computation.1 | async-start | bytes 1835008 | tf_op jit(solution)/shard_map/slice | solution.py:47
  68.0 57.6 %copy-start.2 = (bf16[8,128,2,128]{1,3,2,0:T(8,128)(2,1)S(1)}, bf16[8,128,2,128]{1,3,2,0:T(8,128)(2,1)}, u32[]{:S(2)}) copy-start(bf16[8,128,2,128]{1,3,2,0:T(8,128)(2,1)} %copy-done.1) | copy-start | bytes 1572868
  100.9 53.3 %copy-start.6 = (f32[256]{0:T(256)S(1)}, f32[256]{0:T(256)}, u32[]{:S(2)}) copy-start(f32[256]{0:T(256)} %param.13) | copy-start | bytes 3076
Sparse Core Ops, SparseCore 0:
  12.8 88.0 all-gather.1
where the time goes:
time: 167 us; the launch traced here: 166 us
  other arithmetic  40.8 us (24%)
  waiting for transfers between devices  32.9 us (20%)
  local copies, waits for them, and re-layouts  31 us (19%)
  blocking collectives  26.7 us (16%)
  between operations  13.6 us (8%)
  starting transfers between devices  12 us (7%)
  matrix products  8.16 us (5%)
    all_gather x1, waiting for transfers between devices, carried_in(): gathered = lax.all_gather(part, axis)  32.9 us
    psum x1, blocking collectives, shards(): row_squares = lax.psum(local_squares, 'outer')  26.7 us
    add x24, other arithmetic, add_states(): return earlier + later  22.5 us
    another operation x8, local copies, waits for them, and re-layouts, shards(): jnp.stack([extended_values[place:place + groups_here] for place in range(...  13.2 us
    ppermute x3, starting transfers between devices, from_behind(): lax.ppermute(value, axis, [(source, source + steps) for source in range(f...  12 us
    another operation x8, local copies, waits for them, and re-layouts, shards(): jnp.stack([extended_keys[place:place + groups_here] for place in range(PR...  7.08 us
    another operation x1, other arithmetic, shards(): jnp.stack([extended_values[place:place + groups_here] for place in range(...  6.43 us
    sub x1, other arithmetic, shards(): expd = jnp.exp(scores - largest)  3.88 us
  transfers between devices with their start and end apart: 4, of which 1 were waited for; matrix products, arithmetic and copies ran while one was open for 26% of the time, Pallas kernels for 0%

commit v1 on v0

v1 whole, which is shorter than its diff:
```python
import functools

import jax
import jax.numpy as jnp
from jax import lax
from jax.experimental import pallas as pl
from jax.experimental.pallas import tpu as pltpu
from jax.sharding import PartitionSpec as P

HD = 128
BLK = 128
PREV = 3
MESH = pl.DeviceIdType.MESH
NEG = -1e30
LOG2E = 1.4426950408889634


def dot_nt(a, b):
    return lax.dot_general(a, b, (((1,), (1,)), ((), ())), preferred_element_type=jnp.float32)


def dot_tn(a, b):
    return lax.dot_general(a, b, (((0,), (0,)), ((), ())), preferred_element_type=jnp.float32)


def dot_nn(a, b):
    return lax.dot_general(a, b, (((1,), (0,)), ((), ())), preferred_element_type=jnp.float32)


def kernel(
    ni,
    no,
    groups,
    heads,
    split,
    counts_ref,
    mask_ref,
    gain_ref,
    q_hbm,
    k_hbm,
    v_hbm,
    o_hbm,
    q_all,
    k_ext,
    v_ext,
    within,
    total,
    parts,
    prefixes,
    before,
    bias,
    rim_out,
    rim_in,
    lin,
    local,
    squares,
    all_squares,
    scale,
    out,
    load_sem,
    store_sem,
    parts_send,
    parts_recv,
    prefix_send,
    prefix_recv,
    rim_send,
    rim_recv,
    square_send,
    square_recv,
):
    rim = PREV * BLK
    span = groups * BLK
    width = no * heads * HD
    here = lax.axis_index("inner")
    stripe = lax.axis_index("outer")
    following = lax.rem(here + 1, ni)

    loads = [
        pltpu.make_async_copy(k_hbm, k_ext.at[pl.ds(rim, span)], load_sem.at[0]),
        pltpu.make_async_copy(v_hbm, v_ext.at[pl.ds(rim, span)], load_sem.at[1]),
        pltpu.make_async_copy(q_hbm, q_all, load_sem.at[2]),
    ]
    for load in loads:
        load.start()

    barrier = pltpu.get_barrier_semaphore()

    @pl.loop(1, ni)
    def _(step):
        pl.semaphore_signal(
            barrier, inc=1, device_id={"inner": lax.rem(here + step, ni)}, device_id_type=MESH
        )

    @pl.loop(1, no)
    def _(step):
        pl.semaphore_signal(
            barrier, inc=1, device_id={"outer": lax.rem(stripe + step, no)}, device_id_type=MESH
        )

    lane = lax.broadcasted_iota(jnp.int32, (1, BLK), 1)
    for g in range(groups):
        bias[pl.ds(g, 1), :] = jnp.where(lane < counts_ref[g], 0.0, NEG)
    rim_out[...] = jnp.full(rim_out.shape, NEG, jnp.float32)
    for j in range(PREV):
        rim_out[pl.ds(j, 1), :] = bias[pl.ds(groups - PREV + j, 1), :]

    loads[0].wait()
    loads[1].wait()
    token = lax.broadcasted_iota(jnp.int32, (BLK, HD), 0)
    for h in range(heads):
        cols = pl.ds(h * HD, HD)
        running = jnp.zeros((HD, HD), jnp.float32)
        for g in range(groups):
            rows = pl.ds(rim + g * BLK, BLK)
            masked = jnp.where(token < counts_ref[g], k_ext[rows, cols], jnp.zeros((), jnp.bfloat16))
            within[g, cols, :] = running
            running = running + dot_tn(masked, v_ext[rows, cols])
        piece = heads * HD // ni
        each = ni // heads
        total[pl.ds(h * each, each)] = running.reshape(each, piece, HD)
    parts[pl.ds(here, 1)] = total[pl.ds(here, 1)]

    pl.semaphore_wait(barrier, ni - 1 + no - 1)

    @pl.loop(1, ni)
    def _(step):
        there = lax.rem(here + step, ni)
        pltpu.make_async_remote_copy(
            src_ref=total.at[there],
            dst_ref=parts.at[here],
            send_sem=parts_send,
            recv_sem=parts_recv,
            device_id={"inner": there},
            device_id_type=MESH,
        ).start()

    rims = [
        pltpu.make_async_remote_copy(
            src_ref=source,
            dst_ref=target,
            send_sem=rim_send.at[n],
            recv_sem=rim_recv.at[n],
            device_id={"inner": following},
            device_id_type=MESH,
        )
        for n, (source, target) in enumerate(
            (
                (rim_out, rim_in),
                (k_ext.at[pl.ds(span, rim)], k_ext.at[pl.ds(0, rim)]),
                (v_ext.at[pl.ds(span, rim)], v_ext.at[pl.ds(0, rim)]),
            )
        )
    ]
    for copy in rims:
        copy.start()

    loads[2].wait()
    causal = lax.broadcasted_iota(jnp.int32, (BLK, BLK), 0) >= lax.broadcasted_iota(
        jnp.int32, (BLK, BLK), 1
    )
    factor = LOG2E / HD**0.5

    def intra(g, scores, h):
        valid = causal & (bias[pl.ds(g, 1), :] == 0.0)
        weights = jnp.where(valid, scores, 0.0).astype(jnp.bfloat16)
        rows = pl.ds(g * BLK, BLK)
        lin[rows, pl.ds(h * HD, HD)] = dot_nn(
            weights, v_ext[pl.ds(rim + g * BLK, BLK), pl.ds(h * HD, HD)]
        )

    def window(g, earlier, with_intra):
        rows = pl.ds(g * BLK, BLK)
        for h in range(heads):
            cols = pl.ds(h * HD, HD)
            keys = pl.ds(g * BLK, (PREV + 1) * BLK)
            scores = dot_nt(q_all[rows, cols], k_ext[keys, cols])
            own = scores[:, PREV * BLK :]
            if with_intra:
                intra(g, own, h)
            seen = [scores[:, j * BLK : (j + 1) * BLK] + earlier[j] for j in range(PREV)]
            seen.append(jnp.where(causal, own + bias[pl.ds(g, 1), :], NEG))
            largest = functools.reduce(jnp.maximum, seen)
            largest = jnp.max(largest, axis=-1, keepdims=True)
            expd = [jnp.exp2((s - largest) * factor) for s in seen]
            denominator = jnp.sum(functools.reduce(jnp.add, expd), axis=-1, keepdims=True)
            inverse = 1.0 / denominator
            weights = jnp.concatenate([(e * inverse).astype(jnp.bfloat16) for e in expd], axis=1)
            local[rows, cols] = dot_nn(weights, v_ext[keys, cols])

    def switch(g, j):
        return jnp.where(mask_ref[g, PREV - 1 - j] == 1, 0.0, NEG)

    def inner_window(g):
        window(g, [bias[pl.ds(g - PREV + j, 1), :] + switch(g, j) for j in range(PREV)], True)

    @pl.loop(PREV, split)
    def _(g):
        inner_window(g)

    def arrived(buffer, send, recv, count):
        return pltpu.make_async_remote_copy(
            src_ref=buffer.at[pl.ds(0, count)],
            dst_ref=buffer.at[pl.ds(0, count)],
            send_sem=send,
            recv_sem=recv,
            device_id={"inner": following},
            device_id_type=MESH,
        )

    arrived(parts, parts_send, parts_recv, ni - 1).wait_recv()
    so_far = jnp.zeros(parts.shape[1:], jnp.float32)
    for n in range(ni):
        prefixes[n] = so_far
        so_far = so_far + parts[n]
    before[pl.ds(here, 1)] = prefixes[pl.ds(here, 1)]

    @pl.loop(1, ni)
    def _(step):
        there = lax.rem(here + step, ni)
        pltpu.make_async_remote_copy(
            src_ref=prefixes.at[there],
            dst_ref=before.at[here],
            send_sem=prefix_send,
            recv_sem=prefix_recv,
            device_id={"inner": there},
            device_id_type=MESH,
        ).start()

    @pl.loop(split, groups)
    def _(g):
        inner_window(g)

    @pl.loop(0, PREV)
    def _(g):
        for h in range(heads):
            cols = pl.ds(h * HD, HD)
            intra(
                g,
                dot_nt(q_all[pl.ds(g * BLK, BLK), cols], k_ext[pl.ds(rim + g * BLK, BLK), cols]),
                h,
            )

    arrived(before, prefix_send, prefix_recv, ni - 1).wait_recv()

    @pl.loop(0, groups)
    def _(g):
        rows = pl.ds(g * BLK, BLK)
        powers = jnp.zeros((BLK, HD), jnp.float32)
        for h in range(heads):
            cols = pl.ds(h * HD, HD)
            each = ni // heads
            carried = before[pl.ds(h * each, each)].reshape(HD, HD)
            prior = (carried + within[g, cols, :]).astype(jnp.bfloat16)
            whole = lin[rows, cols] + dot_nn(q_all[rows, cols], prior)
            lin[rows, cols] = whole
            powers = powers + whole * whole
        squares[pl.ds(g, 1), :] = jnp.sum(powers.T, axis=0, keepdims=True)

    all_squares[pl.ds(stripe, 1)] = squares[...][None]

    @pl.loop(1, no)
    def _(step):
        there = lax.rem(stripe + step, no)
        pltpu.make_async_remote_copy(
            src_ref=squares,
            dst_ref=all_squares.at[stripe],
            send_sem=square_send,
            recv_sem=square_recv,
            device_id={"outer": there},
            device_id_type=MESH,
        ).start()

    for copy in rims:
        copy.wait_recv()
    first = jnp.where(here == 0, NEG, 0.0)

    @pl.loop(0, PREV)
    def _(g):
        earlier = []
        for j in range(PREV):
            row = g - PREV + j
            behind = rim_in[pl.ds(jnp.minimum(row + PREV, PREV), 1), :] + first
            inside = bias[pl.ds(jnp.maximum(row, 0), 1), :]
            earlier.append(jnp.where(row < 0, behind, inside) + switch(g, j))
        window(g, earlier, False)

    arrived(all_squares, square_send, square_recv, no - 1).wait_recv()
    row_squares = jnp.sum(all_squares[...], axis=0)
    scale[...] = lax.rsqrt(row_squares / width + 1e-6)

    @pl.loop(0, groups)
    def _(g):
        rows = pl.ds(g * BLK, BLK)
        by_token = jnp.broadcast_to(scale[pl.ds(g, 1), :], (HD, BLK)).T
        for h in range(heads):
            cols = pl.ds(h * HD, HD)
            normed = lin[rows, cols] * by_token
            out[rows, cols] = (normed * gain_ref[:, cols] + local[rows, cols]).astype(jnp.bfloat16)

    store = pltpu.make_async_copy(out, o_hbm, store_sem)
    store.start()
    arrived(total, parts_send, parts_recv, ni - 1).wait_send()
    arrived(prefixes, prefix_send, prefix_recv, ni - 1).wait_send()
    arrived(all_squares, square_send, square_recv, no - 1).wait_send()
    for copy in rims:
        copy.wait_send()
    store.wait()


def shards(ni, no, queries, keys, values, counts, window_mask, norm_gain):
    span, wide = queries.shape
    groups, heads = span // BLK, wide // HD
    piece = heads * HD // ni
    rim = PREV * BLK
    any_space = pl.BlockSpec(memory_space=pl.ANY)
    dma = pltpu.SemaphoreType.DMA
    f32, bf16 = jnp.float32, jnp.bfloat16
    return pl.pallas_call(
        functools.partial(kernel, ni, no, groups, heads, min(groups, PREV + 3)),
        out_shape=jax.ShapeDtypeStruct((span, wide), bf16),
        in_specs=[
            pl.BlockSpec(memory_space=pltpu.SMEM),
            pl.BlockSpec(memory_space=pltpu.SMEM),
            pl.BlockSpec(memory_space=pltpu.VMEM),
            any_space,
            any_space,
            any_space,
        ],
        out_specs=any_space,
        scratch_shapes=[
            pltpu.VMEM((span, wide), bf16),
            pltpu.VMEM((rim + span, wide), bf16),
            pltpu.VMEM((rim + span, wide), bf16),
            pltpu.VMEM((groups, heads * HD, HD), f32),
            pltpu.VMEM((ni, piece, HD), f32),
            pltpu.VMEM((ni, piece, HD), f32),
            pltpu.VMEM((ni, piece, HD), f32),
            pltpu.VMEM((ni, piece, HD), f32),
            pltpu.VMEM((groups, BLK), f32),
            pltpu.VMEM((8, BLK), f32),
            pltpu.VMEM((8, BLK), f32),
            pltpu.VMEM((span, wide), f32),
            pltpu.VMEM((span, wide), f32),
            pltpu.VMEM((groups, BLK), f32),
            pltpu.VMEM((no, groups, BLK), f32),
            pltpu.VMEM((groups, BLK), f32),
            pltpu.VMEM((span, wide), bf16),
            dma((3,)),
            dma,
            dma,
            dma,
            dma,
            dma,
            dma((3,)),
            dma((3,)),
            dma,
            dma,
        ],
        compiler_params=pltpu.CompilerParams(
            collective_id=0, has_side_effects=True, vmem_limit_bytes=48 * 2**20
        ),
        name="layer",
    )(counts, window_mask, norm_gain.reshape(1, wide), queries, keys, values)


def solution(mesh):
    return jax.shard_map(
        functools.partial(shards, mesh.shape["inner"], mesh.shape["outer"]),
        mesh=mesh,
        in_specs=(
            P("inner", "outer"),
            P("inner", "outer"),
            P("inner", "outer"),
            P("inner"),
            P("inner", None),
            P("outer"),
        ),
        out_specs=P("inner", "outer"),
        check_vma=False,
    )
```

time: 167 us -> 47 us (0.28)
  the two profiles are of different devices: /device:TPU:7 before, /device:TPU:1 now
where the time goes in v1:
time: 47 us; the launch traced here: 46.7 us
  Pallas kernels  42 us (89%)
  local copies, waits for them, and re-layouts  4.71 us (10%)
    pallas_call x1, Pallas kernels, shards(): pl.pallas_call(functools.partial(kernel, ni, no, groups, heads, min(group...  42 us
    unnamed x12, local copies, waits for them, and re-layouts  4.71 us

profile of v1, /device:TPU:1, one launch (start us, length us, event | category | flops | bytes accessed | tf_op | source)
XLA Modules:
  0.0 46.7 jit_solution(14084407420568609651)
XLA Ops:
  0.0 0.0 copy-start.3
  0.0 0.0 copy-start.4
  0.0 0.8 %copy.7.mask_ref = s32[8,3]{1,0:T(8,128)S(1)} copy(s32[8,3]{0,1:T(4,128)} %param.10) | data formatting | bytes 192 | tf_op args[4]
  0.8 0.0 copy-done.3
  0.8 0.0 copy-done.4
  0.8 0.0 copy-start
  0.8 1.0 %copy-done = bf16[1024,256]{1,0:T(8,128)(2,1)S(1)} copy-done((bf16[1024,256]{1,0:T(8,128)(2,1)S(1)}, bf16[1024,256]{1,0:T(8,128)(2,1)}, u32[]{:S(2)}) %copy-start) | copy-done | bytes 524312
  1.8 0.0 copy-start.1
  1.8 1.0 %copy-done.1 = bf16[1024,256]{1,0:T(8,128)(2,1)S(1)} copy-done((bf16[1024,256]{1,0:T(8,128)(2,1)S(1)}, bf16[1024,256]{1,0:T(8,128)(2,1)}, u32[]{:S(2)}) %copy-start.1) | copy-done | bytes 524312
  2.9 0.0 copy-start.2
  2.9 1.0 %copy-done.2 = bf16[1024,256]{1,0:T(8,128)(2,1)S(1)} copy-done((bf16[1024,256]{1,0:T(8,128)(2,1)S(1)}, bf16[1024,256]{1,0:T(8,128)(2,1)}, u32[]{:S(2)}) %copy-start.2) | copy-done | bytes 524312
  3.9 42.0 %layer.1 = bf16[1024,256]{1,0:T(8,128)(2,1)S(1)} custom-call(s32[8]{0:T(128)S(1)} %copy-done.4, s32[8,3]{1,0:T(8,128)S(1)} %copy.7.mask_ref, f32[1,256]{1,0:T(1,128)S(1)} %bitcast.1, bf16[1024,256]{1,0:T(8,128)(2,1)S(1)} %copy-done, bf16[1024,256]{1,0:T(8,128)(2,1)S(1)} %copy-done.1, bf16[1024,256]{1,0:T(8,128)(2,1)S(1)} %copy-done.2), custom_call_target="tpu_custom_call" | custom-call | tf_op jit(solution)/shard_map/layer/pallas_call | solution.py:318
  45.9 0.8 %copy.9 = bf16[1024,256]{1,0:T(8,128)(2,1)} copy(bf16[1024,256]{1,0:T(8,128)(2,1)S(1)} %layer.1) | data formatting | bytes 1048576
Async XLA Ops:
  0.0 0.8 %copy-start.3 = (f32[256]{0:T(256)S(1)}, f32[256]{0:T(256)}, u32[]{:S(2)}) copy-start(f32[256]{0:T(256)} %param.11) | copy-start | bytes 3076
  0.0 0.8 %copy-start.4 = (s32[8]{0:T(128)S(1)}, s32[8]{0:T(128)}, u32[]{:S(2)}) copy-start(s32[8]{0:T(128)} %counts_ref.1) | copy-start | bytes 100
  0.8 1.0 %copy-start = (bf16[1024,256]{1,0:T(8,128)(2,1)S(1)}, bf16[1024,256]{1,0:T(8,128)(2,1)}, u32[]{:S(2)}) copy-start(bf16[1024,256]{1,0:T(8,128)(2,1)} %q_hbm.1) | copy-start | bytes 1572868
  1.8 1.0 %copy-start.1 = (bf16[1024,256]{1,0:T(8,128)(2,1)S(1)}, bf16[1024,256]{1,0:T(8,128)(2,1)}, u32[]{:S(2)}) copy-start(bf16[1024,256]{1,0:T(8,128)(2,1)} %k_hbm.1) | copy-start | bytes 1572868
  2.9 1.0 %copy-start.2 = (bf16[1024,256]{1,0:T(8,128)(2,1)S(1)}, bf16[1024,256]{1,0:T(8,128)(2,1)}, u32[]{:S(2)}) copy-start(bf16[1024,256]{1,0:T(8,128)(2,1)} %v_hbm.1) | copy-start | bytes 1572868

commit v2 on v1

v2 whole, which is shorter than its diff:
```python
import functools

import jax
import jax.numpy as jnp
from jax import lax
from jax.experimental import pallas as pl
from jax.experimental.pallas import tpu as pltpu
from jax.sharding import PartitionSpec as P

HD = 128
BLK = 128
PREV = 3
LOADS = 4
MESH = pl.DeviceIdType.MESH
NEG = -1e30
LOG2E = 1.4426950408889634


def torus(sizes):
    def hops(step):
        return sum(min(s, n - s) for s, n in zip(step, sizes))

    steps = [()]
    for n in sizes:
        steps = [(*step, s) for step in steps for s in range(n)]
    return sorted(steps[1:], key=hops, reverse=True)


def moved(place, step, sizes):
    index, stride = 0, 1
    for s, n in zip(reversed(step), reversed(sizes)):
        digit = lax.rem(place // stride, n) if stride > 1 else lax.rem(place, n)
        index = index + lax.rem(digit + s, n) * stride
        stride *= n
    return index


def dot_nt(a, b):
    return lax.dot_general(a, b, (((1,), (1,)), ((), ())), preferred_element_type=jnp.float32)


def dot_tn(a, b):
    return lax.dot_general(a, b, (((0,), (0,)), ((), ())), preferred_element_type=jnp.float32)


def dot_nn(a, b):
    return lax.dot_general(a, b, (((1,), (0,)), ((), ())), preferred_element_type=jnp.float32)


def kernel(
    ni,
    no,
    groups,
    heads,
    counts_hbm,
    mask_hbm,
    gain_hbm,
    q_hbm,
    k_hbm,
    v_hbm,
    o_hbm,
    counts_ref,
    mask_ref,
    gain_ref,
    q_all,
    k_ext,
    v_ext,
    within,
    total,
    parts,
    prefixes,
    before,
    bias,
    rim_out,
    rim_in,
    lin,
    local,
    squares,
    all_squares,
    scale,
    out,
    small_sem,
    load_sem,
    store_sem,
    parts_send,
    parts_recv,
    prefix_send,
    prefix_recv,
    rim_send,
    rim_recv,
    square_send,
    square_recv,
    ready,
):
    rim = PREV * BLK
    span = groups * BLK
    width = no * heads * HD
    here = lax.axis_index("inner")
    stripe = lax.axis_index("outer")
    following = lax.rem(here + 1, ni)

    small = [
        pltpu.make_async_copy(counts_hbm, counts_ref, small_sem.at[0]),
        pltpu.make_async_copy(mask_hbm, mask_ref, small_sem.at[1]),
        pltpu.make_async_copy(gain_hbm, gain_ref, small_sem.at[2]),
    ]
    chunk = span // LOADS
    loads = []
    for n in range(LOADS):
        rows, ext = pl.ds(n * chunk, chunk), pl.ds(rim + n * chunk, chunk)
        loads.append(pltpu.make_async_copy(k_hbm.at[rows], k_ext.at[ext], load_sem.at[2 * n]))
        loads.append(pltpu.make_async_copy(v_hbm.at[rows], v_ext.at[ext], load_sem.at[2 * n + 1]))
    load_q = pltpu.make_async_copy(q_hbm, q_all, load_sem.at[2 * LOADS])
    small[0].start()
    for load in loads:
        load.start()
    small[1].start()
    small[2].start()
    load_q.start()

    barrier = pltpu.get_barrier_semaphore()
    inner_sizes = (4, 8) if ni == 32 else (ni,)
    outer_sizes = (8, 2) if no == 16 else (no,)
    inner_peers = [{"inner": moved(here, step, inner_sizes)} for step in torus(inner_sizes)]
    outer_peers = [{"outer": moved(stripe, step, outer_sizes)} for step in torus(outer_sizes)]
    line = inner_sizes[-1]
    half = line // 2
    owners = ni // 2

    def owns(place):
        return lax.rem(place, line) < half

    def rank(place):
        return place // line * half + lax.rem(place, line)

    owner = owns(here)
    preceding = lax.rem(here + ni - 1, ni)

    @pl.when(owner)
    def _():
        for peer in inner_peers:
            pl.semaphore_signal(barrier, inc=1, device_id=peer, device_id_type=MESH)

    @pl.when(jnp.logical_not(owner))
    def _():
        pl.semaphore_signal(barrier, inc=1, device_id={"inner": preceding}, device_id_type=MESH)

    for peer in outer_peers:
        pl.semaphore_signal(barrier, inc=1, device_id=peer, device_id_type=MESH)

    small[0].wait()
    lane = lax.broadcasted_iota(jnp.int32, (1, BLK), 1)
    for g in range(groups):
        bias[pl.ds(g, 1), :] = jnp.where(lane < counts_ref[g], 0.0, NEG)
    rim_out[...] = jnp.full(rim_out.shape, NEG, jnp.float32)
    for j in range(PREV):
        rim_out[pl.ds(j, 1), :] = bias[pl.ds(groups - PREV + j, 1), :]

    token = lax.broadcasted_iota(jnp.int32, (BLK, HD), 0)
    each = owners // heads
    piece = heads * HD // owners
    running = [jnp.zeros((HD, HD), jnp.float32)] * heads
    for g in range(groups):
        if (g * BLK) % chunk == 0:
            loads[2 * (g * BLK // chunk)].wait()
            loads[2 * (g * BLK // chunk) + 1].wait()
        for h in range(heads):
            cols = pl.ds(h * HD, HD)
            rows = pl.ds(rim + g * BLK, BLK)
            masked = jnp.where(token < counts_ref[g], k_ext[rows, cols], jnp.zeros((), jnp.bfloat16))
            if g:
                within[g, cols, :] = running[h].astype(jnp.bfloat16)
            running[h] = running[h] + dot_tn(masked, v_ext[rows, cols])
    for h in range(heads):
        total[pl.ds(h * each, each)] = running[h].reshape(each, piece, HD).astype(jnp.bfloat16)
    within[0] = jnp.zeros(within.shape[1:], jnp.bfloat16)

    pl.semaphore_wait(
        barrier,
        no - 1 + owners - jnp.where(owner, 1, 0) + jnp.where(owns(following), 0, 1),
    )

    def send_part(peer):
        there = peer["inner"]

        @pl.when(owns(there))
        def _():
            pltpu.make_async_remote_copy(
                src_ref=total.at[rank(there)],
                dst_ref=parts.at[here],
                send_sem=parts_send,
                recv_sem=parts_recv,
                device_id=peer,
                device_id_type=MESH,
            ).start()

    for peer in inner_peers:
        send_part(peer)

    rims = [
        pltpu.make_async_remote_copy(
            src_ref=source,
            dst_ref=target,
            send_sem=rim_send.at[n],
            recv_sem=rim_recv.at[n],
            device_id={"inner": following},
            device_id_type=MESH,
        )
        for n, (source, target) in enumerate(
            (
                (rim_out, rim_in),
                (k_ext.at[pl.ds(span, rim)], k_ext.at[pl.ds(0, rim)]),
                (v_ext.at[pl.ds(span, rim)], v_ext.at[pl.ds(0, rim)]),
            )
        )
    ]
    first, last = here == 0, here == ni - 1

    @pl.when(jnp.logical_not(last))
    def _():
        for copy in rims:
            copy.start()

    @pl.when(first)
    def _():
        rim_in[...] = jnp.full(rim_in.shape, NEG, jnp.float32)
        k_ext[pl.ds(0, rim)] = jnp.zeros((rim, k_ext.shape[1]), jnp.bfloat16)
        v_ext[pl.ds(0, rim)] = jnp.zeros((rim, v_ext.shape[1]), jnp.bfloat16)

    @pl.when(jnp.logical_not(owner))
    def _():
        for n in range(owners):
            pl.semaphore_signal(
                ready,
                inc=1,
                device_id={"inner": n // half * line + n % half},
                device_id_type=MESH,
            )

    load_q.wait()
    small[1].wait()
    causal = lax.broadcasted_iota(jnp.int32, (BLK, BLK), 0) >= lax.broadcasted_iota(
        jnp.int32, (BLK, BLK), 1
    )
    factor = LOG2E / HD**0.5

    def intra(g, scores, h):
        valid = causal & (bias[pl.ds(g, 1), :] == 0.0)
        weights = jnp.where(valid, scores, 0.0).astype(jnp.bfloat16)
        rows, cols = pl.ds(g * BLK, BLK), pl.ds(h * HD, HD)
        lin[rows, cols] = dot_nn(weights, v_ext[pl.ds(rim + g * BLK, BLK), cols]) + dot_nn(
            q_all[rows, cols], within[g, cols, :]
        )

    def window(g, earlier, with_intra):
        rows = pl.ds(g * BLK, BLK)
        for h in range(heads):
            cols = pl.ds(h * HD, HD)
            keys = pl.ds(g * BLK, (PREV + 1) * BLK)
            scores = dot_nt(q_all[rows, cols], k_ext[keys, cols])
            own = scores[:, PREV * BLK :]
            if with_intra:
                intra(g, own, h)
            seen = [scores[:, j * BLK : (j + 1) * BLK] + earlier[j] for j in range(PREV)]
            seen.append(jnp.where(causal, own + bias[pl.ds(g, 1), :], NEG))
            largest = functools.reduce(jnp.maximum, seen)
            largest = jnp.max(largest, axis=-1, keepdims=True)
            expd = [jnp.exp2((s - largest) * factor) for s in seen]
            denominator = jnp.sum(functools.reduce(jnp.add, expd), axis=-1, keepdims=True)
            inverse = 1.0 / denominator
            weights = jnp.concatenate([(e * inverse).astype(jnp.bfloat16) for e in expd], axis=1)
            local[rows, cols] = dot_nn(weights, v_ext[keys, cols])

    def switch(g, j):
        return jnp.where(mask_ref[PREV - 1 - j, g] == 1, 0.0, NEG)

    def inner_window(g):
        window(g, [bias[pl.ds(g - PREV + j, 1), :] + switch(g, j) for j in range(PREV)], True)

    @pl.loop(PREV, groups)
    def _(g):
        inner_window(g)

    def arrived(buffer, send, recv, count):
        return pltpu.make_async_remote_copy(
            src_ref=buffer.at[pl.ds(0, count)],
            dst_ref=buffer.at[pl.ds(0, count)],
            send_sem=send,
            recv_sem=recv,
            device_id={"inner": following},
            device_id_type=MESH,
        )

    @pl.loop(0, PREV)
    def _(g):
        for h in range(heads):
            cols = pl.ds(h * HD, HD)
            intra(
                g,
                dot_nt(q_all[pl.ds(g * BLK, BLK), cols], k_ext[pl.ds(rim + g * BLK, BLK), cols]),
                h,
            )

    @pl.when(owner)
    def _():
        parts[pl.ds(here, 1)] = total[pl.ds(rank(here), 1)]
        arrived(parts, parts_send, parts_recv, ni - 1).wait_recv()
        so_far = jnp.zeros(parts.shape[1:], jnp.float32)
        for n in range(ni):
            prefixes[n] = so_far.astype(jnp.bfloat16)
            so_far = so_far + parts[n].astype(jnp.float32)
        before[pl.ds(rank(here), 1)] = prefixes[pl.ds(here, 1)]
        pl.semaphore_wait(ready, ni - owners)
        for peer in inner_peers:
            pltpu.make_async_remote_copy(
                src_ref=prefixes.at[peer["inner"]],
                dst_ref=before.at[rank(here)],
                send_sem=prefix_send,
                recv_sem=prefix_recv,
                device_id=peer,
                device_id_type=MESH,
            ).start()


    @pl.when(owner)
    def _():
        arrived(before, prefix_send, prefix_recv, owners - 1).wait_recv()

    @pl.when(jnp.logical_not(owner))
    def _():
        arrived(before, prefix_send, prefix_recv, owners).wait_recv()


    carried = [
        before[pl.ds(h * each, each)].reshape(HD, HD) for h in range(heads)
    ]
    for g in range(groups):
        rows = pl.ds(g * BLK, BLK)
        powers = jnp.zeros((BLK, HD), jnp.float32)
        for h in range(heads):
            cols = pl.ds(h * HD, HD)
            whole = lin[rows, cols] + dot_nn(q_all[rows, cols], carried[h])
            lin[rows, cols] = whole
            powers = powers + whole * whole
        squares[pl.ds(g, 1), :] = jnp.sum(powers.T, axis=0, keepdims=True)

    all_squares[pl.ds(stripe, 1)] = squares[...][None]

    for peer in outer_peers:
        pltpu.make_async_remote_copy(
            src_ref=squares,
            dst_ref=all_squares.at[stripe],
            send_sem=square_send,
            recv_sem=square_recv,
            device_id=peer,
            device_id_type=MESH,
        ).start()


    @pl.when(jnp.logical_not(first))
    def _():
        for copy in rims:
            copy.wait_recv()

    @pl.loop(0, PREV)
    def _(g):
        earlier = []
        for j in range(PREV):
            row = g - PREV + j
            behind = rim_in[pl.ds(jnp.minimum(row + PREV, PREV), 1), :]
            inside = bias[pl.ds(jnp.maximum(row, 0), 1), :]
            earlier.append(jnp.where(row < 0, behind, inside) + switch(g, j))
        window(g, earlier, False)

    arrived(all_squares, square_send, square_recv, no - 1).wait_recv()
    row_squares = jnp.sum(all_squares[...], axis=0)
    scale[...] = lax.rsqrt(row_squares / width + 1e-6)

    small[2].wait()
    stores = []
    for g in range(groups):
        rows = pl.ds(g * BLK, BLK)
        by_token = jnp.broadcast_to(scale[pl.ds(g, 1), :], (HD, BLK)).T
        for h in range(heads):
            cols = pl.ds(h * HD, HD)
            normed = lin[rows, cols] * by_token
            out[rows, cols] = (normed * gain_ref[:, cols] + local[rows, cols]).astype(jnp.bfloat16)
        stores.append(pltpu.make_async_copy(out.at[rows], o_hbm.at[rows], store_sem.at[g]))
        stores[-1].start()


    @pl.when(owner)
    def _():
        arrived(total, parts_send, parts_recv, owners - 1).wait_send()
        arrived(prefixes, prefix_send, prefix_recv, ni - 1).wait_send()

    @pl.when(jnp.logical_not(owner))
    def _():
        arrived(total, parts_send, parts_recv, owners).wait_send()

    arrived(all_squares, square_send, square_recv, no - 1).wait_send()

    @pl.when(jnp.logical_not(last))
    def _():
        for copy in rims:
            copy.wait_send()

    for store in stores:
        store.wait()


def shards(ni, no, queries, keys, values, counts, window_mask, norm_gain):
    span, wide = queries.shape
    groups, heads = span // BLK, wide // HD
    owners = ni // 2
    piece = heads * HD // owners
    rim = PREV * BLK
    any_space = pl.BlockSpec(memory_space=pltpu.HBM)
    dma = pltpu.SemaphoreType.DMA
    f32, bf16 = jnp.float32, jnp.bfloat16
    return pl.pallas_call(
        functools.partial(kernel, ni, no, groups, heads),
        out_shape=jax.ShapeDtypeStruct((span, wide), bf16),
        in_specs=[any_space] * 6,
        out_specs=any_space,
        scratch_shapes=[
            pltpu.SMEM(counts.shape, jnp.int32),
            pltpu.SMEM(window_mask.shape[::-1], jnp.int32),
            pltpu.VMEM((1, wide), f32),
            pltpu.VMEM((span, wide), bf16),
            pltpu.VMEM((rim + span, wide), bf16),
            pltpu.VMEM((rim + span, wide), bf16),
            pltpu.VMEM((groups, heads * HD, HD), bf16),
            pltpu.VMEM((owners, piece, HD), bf16),
            pltpu.VMEM((ni, piece, HD), bf16),
            pltpu.VMEM((ni, piece, HD), bf16),
            pltpu.VMEM((owners, piece, HD), bf16),
            pltpu.VMEM((groups, BLK), f32),
            pltpu.VMEM((8, BLK), f32),
            pltpu.VMEM((8, BLK), f32),
            pltpu.VMEM((span, wide), f32),
            pltpu.VMEM((span, wide), f32),
            pltpu.VMEM((groups, BLK), f32),
            pltpu.VMEM((no, groups, BLK), f32),
            pltpu.VMEM((groups, BLK), f32),
            pltpu.VMEM((span, wide), bf16),
            dma((3,)),
            dma((2 * LOADS + 1,)),
            dma((groups,)),
            dma,
            dma,
            dma,
            dma,
            dma((3,)),
            dma((3,)),
            dma,
            dma,
            pltpu.SemaphoreType.REGULAR,
        ],
        compiler_params=pltpu.CompilerParams(
            collective_id=0, has_side_effects=True, vmem_limit_bytes=56 * 2**20
        ),
        name="layer",
    )(counts, window_mask.T, norm_gain.reshape(1, wide), queries, keys, values)


def solution(mesh):
    return jax.shard_map(
        functools.partial(shards, mesh.shape["inner"], mesh.shape["outer"]),
        mesh=mesh,
        in_specs=(
            P("inner", "outer"),
            P("inner", "outer"),
            P("inner", "outer"),
            P("inner"),
            P("inner", None),
            P("outer"),
        ),
        out_specs=P("inner", "outer"),
        check_vma=False,
    )
```

time: 47 us -> 38.7 us (0.82)
  Pallas kernels: 42 us -> 36.6 us
  local copies, waits for them, and re-layouts: 4.71 us -> 1.87 us
    pallas_call x1, Pallas kernels: 42 us -> 36.6 us  [shards(): pl.pallas_call(functools.partial(kernel, ni, no, groups, heads), out_shap...]
    unnamed x12 -> x1, local copies, waits for them, and re-layouts: 4.71 us -> 1.87 us
where the time goes in v2:
time: 38.7 us; the launch traced here: 38.5 us
  Pallas kernels  36.6 us (95%)
  local copies, waits for them, and re-layouts  1.87 us (5%)
    pallas_call x1, Pallas kernels, shards(): pl.pallas_call(functools.partial(kernel, ni, no, groups, heads), out_shap...  36.6 us
    unnamed x1, local copies, waits for them, and re-layouts  1.87 us

profile of v2, /device:TPU:1, one launch (start us, length us, event | category | flops | bytes accessed | tf_op | source)
XLA Modules:
  0.0 38.5 jit_solution(1342776745164853650)
XLA Ops:
  0.0 36.6 %layer.1 = bf16[1024,256]{1,0:T(8,128)(2,1)} custom-call(s32[8]{0:T(128)} %counts_hbm.1, s32[3,8]{1,0:T(4,128)} %bitcast.2, f32[1,256]{1,0:T(1,128)} %bitcast.3, bf16[1024,256]{1,0:T(8,128)(2,1)} %q_hbm.1, bf16[1024,256]{1,0:T(8,128)(2,1)} %k_hbm.1, bf16[1024,256]{1,0:T(8,128)(2,1)} %v_hbm.1), custom_call_target="tpu_custom_call" | custom-call | tf_op jit(solution)/shard_map/layer/pallas_call | solution.py:421
  36.6 1.9 %copy.8 = bf16[1024,256]{1,0:T(8,128)(2,1)} copy(bf16[1024,256]{1,0:T(8,128)(2,1)} %layer.1) | data formatting | bytes 1048576

commit v3 on v2

--- a/solution.py
+++ b/solution.py
@@ -91,6 +91,13 @@
     square_send,
     square_recv,
     ready,
+    entered,
+    go,
+    relay_bias,
+    relay_keys,
+    relay_values,
+    hop_send,
+    hop_recv,
 ):
     rim = PREV * BLK
     span = groups * BLK
@@ -119,7 +126,7 @@
     load_q.start()
 
     barrier = pltpu.get_barrier_semaphore()
-    inner_sizes = (4, 8) if ni == 32 else (ni,)
+    inner_sizes = {32: (4, 8), 8: (2, 4)}.get(ni, (1, ni))
     outer_sizes = (8, 2) if no == 16 else (no,)
     inner_peers = [{"inner": moved(here, step, inner_sizes)} for step in torus(inner_sizes)]
     outer_peers = [{"outer": moved(stripe, step, outer_sizes)} for step in torus(outer_sizes)]
@@ -135,6 +142,14 @@
 
     owner = owns(here)
     preceding = lax.rem(here + ni - 1, ni)
+    first, last = here == 0, here == ni - 1
+    tail = lax.rem(here, line) == line - 1
+    straight = jnp.logical_not(tail)
+    detour = jnp.logical_and(tail, jnp.logical_not(last))
+    relays = jnp.logical_and(tail, here >= line)
+    ahead = lax.rem(here + line, ni)
+    behind = lax.rem(here + ni - line, ni)
+    head = here // line * line
 
     @pl.when(owner)
     def _():
@@ -145,8 +160,16 @@
     def _():
         pl.semaphore_signal(barrier, inc=1, device_id={"inner": preceding}, device_id_type=MESH)
 
-    for peer in outer_peers:
-        pl.semaphore_signal(barrier, inc=1, device_id=peer, device_id_type=MESH)
+    @pl.when(relays)
+    def _():
+        pl.semaphore_signal(barrier, inc=1, device_id={"inner": behind}, device_id_type=MESH)
+
+    hub = stripe == 0
+
+    @pl.when(hub)
+    def _():
+        for peer in outer_peers:
+            pl.semaphore_signal(barrier, inc=1, device_id=peer, device_id_type=MESH)
 
     small[0].wait()
     lane = lax.broadcasted_iota(jnp.int32, (1, BLK), 1)
@@ -156,14 +179,43 @@
     for j in range(PREV):
         rim_out[pl.ds(j, 1), :] = bias[pl.ds(groups - PREV + j, 1), :]
 
+    greeters = (
+        owners
+        - jnp.where(owner, 1, 0)
+        + jnp.where(owns(following), 0, 1)
+        + jnp.where(detour, 1, 0)
+        + jnp.where(hub, 0, 1)
+    )
+    rims = [(rim_out, rim_in, relay_bias)]
+    for n in reversed(range(PREV)):
+        for ext, relay in ((k_ext, relay_keys), (v_ext, relay_values)):
+            near, far = pl.ds(n * BLK, BLK), pl.ds(span + n * BLK, BLK)
+            rims.append((ext.at[far], ext.at[near], relay.at[near]))
+
+    def push(n, source, target, send, recv, there):
+        return pltpu.make_async_remote_copy(
+            src_ref=source,
+            dst_ref=target,
+            send_sem=send.at[n],
+            recv_sem=recv.at[n],
+            device_id={"inner": there},
+            device_id_type=MESH,
+        )
+
+    for load in loads:
+        load.wait()
+
+    @pl.when(detour)
+    def _():
+        pl.semaphore_wait(barrier, greeters)
+        for n, (source, _, relay) in enumerate(rims):
+            push(n, source, relay, rim_send, hop_recv, ahead).start()
+
     token = lax.broadcasted_iota(jnp.int32, (BLK, HD), 0)
     each = owners // heads
     piece = heads * HD // owners
     running = [jnp.zeros((HD, HD), jnp.float32)] * heads
     for g in range(groups):
-        if (g * BLK) % chunk == 0:
-            loads[2 * (g * BLK // chunk)].wait()
-            loads[2 * (g * BLK // chunk) + 1].wait()
         for h in range(heads):
             cols = pl.ds(h * HD, HD)
             rows = pl.ds(rim + g * BLK, BLK)
@@ -175,10 +227,9 @@
         total[pl.ds(h * each, each)] = running[h].reshape(each, piece, HD).astype(jnp.bfloat16)
     within[0] = jnp.zeros(within.shape[1:], jnp.bfloat16)
 
-    pl.semaphore_wait(
-        barrier,
-        no - 1 + owners - jnp.where(owner, 1, 0) + jnp.where(owns(following), 0, 1),
-    )
+    @pl.when(jnp.logical_not(detour))
+    def _():
+        pl.semaphore_wait(barrier, greeters)
 
     def send_part(peer):
         there = peer["inner"]
@@ -189,43 +240,34 @@
                 src_ref=total.at[rank(there)],
                 dst_ref=parts.at[here],
                 send_sem=parts_send,
-                recv_sem=parts_recv,
+                recv_sem=parts_recv.at[here // stage],
                 device_id=peer,
                 device_id_type=MESH,
             ).start()
 
-    for peer in inner_peers:
-        send_part(peer)
-
-    rims = [
-        pltpu.make_async_remote_copy(
-            src_ref=source,
-            dst_ref=target,
-            send_sem=rim_send.at[n],
-            recv_sem=rim_recv.at[n],
-            device_id={"inner": following},
-            device_id_type=MESH,
-        )
-        for n, (source, target) in enumerate(
-            (
-                (rim_out, rim_in),
-                (k_ext.at[pl.ds(span, rim)], k_ext.at[pl.ds(0, rim)]),
-                (v_ext.at[pl.ds(span, rim)], v_ext.at[pl.ds(0, rim)]),
-            )
-        )
-    ]
-    first, last = here == 0, here == ni - 1
+    stage = max(1, ni // 8)
+    stages = ni // stage
 
     @pl.when(jnp.logical_not(last))
     def _():
-        for copy in rims:
-            copy.start()
+        for peer in inner_peers:
+            send_part(peer)
+
+    @pl.when(straight)
+    def _():
+        for n, (source, target, _) in enumerate(rims):
+            push(n, source, target, rim_send, rim_recv, following).start()
 
     @pl.when(first)
     def _():
         rim_in[...] = jnp.full(rim_in.shape, NEG, jnp.float32)
+        before[...] = jnp.zeros(before.shape, jnp.bfloat16)
         k_ext[pl.ds(0, rim)] = jnp.zeros((rim, k_ext.shape[1]), jnp.bfloat16)
         v_ext[pl.ds(0, rim)] = jnp.zeros((rim, v_ext.shape[1]), jnp.bfloat16)
+
+    @pl.when(jnp.logical_not(hub))
+    def _():
+        pl.semaphore_signal(entered, inc=1, device_id={"outer": 0}, device_id_type=MESH)
 
     @pl.when(jnp.logical_not(owner))
     def _():
@@ -277,6 +319,12 @@
     def inner_window(g):
         window(g, [bias[pl.ds(g - PREV + j, 1), :] + switch(g, j) for j in range(PREV)], True)
 
+    @pl.when(relays)
+    def _():
+        for n, (source, target, relay) in enumerate(rims):
+            push(n, source, relay, rim_send, hop_recv, ahead).wait_recv()
+            push(n, relay, target, hop_send, rim_recv, head).start()
+
     @pl.loop(PREV, groups)
     def _(g):
         inner_window(g)
@@ -301,28 +349,56 @@
                 h,
             )
 
-    @pl.when(owner)
-    def _():
-        parts[pl.ds(here, 1)] = total[pl.ds(rank(here), 1)]
-        arrived(parts, parts_send, parts_recv, ni - 1).wait_recv()
-        so_far = jnp.zeros(parts.shape[1:], jnp.float32)
-        for n in range(ni):
-            prefixes[n] = so_far.astype(jnp.bfloat16)
-            so_far = so_far + parts[n].astype(jnp.float32)
-        before[pl.ds(rank(here), 1)] = prefixes[pl.ds(here, 1)]
-        pl.semaphore_wait(ready, ni - owners)
-        for peer in inner_peers:
+    def send_prefix(n):
+        @pl.when(here != n)
+        def _():
             pltpu.make_async_remote_copy(
-                src_ref=prefixes.at[peer["inner"]],
+                src_ref=prefixes.at[n],
                 dst_ref=before.at[rank(here)],
                 send_sem=prefix_send,
                 recv_sem=prefix_recv,
-                device_id=peer,
+                device_id={"inner": n},
                 device_id_type=MESH,
             ).start()
 
-
     @pl.when(owner)
+    def _():
+        parts[pl.ds(here, 1)] = total[pl.ds(rank(here), 1)]
+        so_far = jnp.zeros(parts.shape[1:], jnp.float32)
+        for n in range(stages):
+            members = stage - (n == stages - 1)
+            mine = here // stage == n
+            for own in range(2):
+                if members > own:
+
+                    @pl.when(mine if own else jnp.logical_not(mine))
+                    def _(n=n, count=members - own):
+                        arrived(parts, parts_send, parts_recv.at[n], count).wait_recv()
+
+            following_spans = range(n * stage + 1, n * stage + members + 1)
+            for m in following_spans:
+                so_far = so_far + parts[m - 1].astype(jnp.float32)
+                prefixes[m] = so_far.astype(jnp.bfloat16)
+            early = [m for m in following_spans if n == 0 and m % line < half]
+            for m in early:
+                send_prefix(m)
+            if n == 0:
+                pl.semaphore_wait(ready, ni - owners)
+            for m in following_spans:
+                if m not in early:
+                    send_prefix(m)
+
+        @pl.when(jnp.logical_not(first))
+        def _():
+            before[pl.ds(rank(here), 1)] = prefixes[pl.ds(here, 1)]
+
+    @pl.when(hub)
+    def _():
+        pl.semaphore_wait(entered, no - 1)
+        for peer in outer_peers:
+            pl.semaphore_signal(go, inc=1, device_id=peer, device_id_type=MESH)
+
+    @pl.when(jnp.logical_and(owner, jnp.logical_not(first)))
     def _():
         arrived(before, prefix_send, prefix_recv, owners - 1).wait_recv()
 
@@ -346,6 +422,11 @@
 
     all_squares[pl.ds(stripe, 1)] = squares[...][None]
 
+    @pl.when(jnp.logical_not(hub))
+    def _():
+        pl.semaphore_wait(go, 1)
+
+
     for peer in outer_peers:
         pltpu.make_async_remote_copy(
             src_ref=squares,
@@ -357,19 +438,22 @@
         ).start()
 
 
-    @pl.when(jnp.logical_not(first))
-    def _():
-        for copy in rims:
-            copy.wait_recv()
-
-    @pl.loop(0, PREV)
-    def _(g):
+    def rim_here(n):
+        source, target, _ = rims[n]
+
+        @pl.when(jnp.logical_not(first))
+        def _():
+            push(n, source, target, rim_send, rim_recv, following).wait_recv()
+
+    rim_here(0)
+    for g in reversed(range(PREV)):
+        rim_here(2 * (PREV - g) - 1)
+        rim_here(2 * (PREV - g))
         earlier = []
         for j in range(PREV):
             row = g - PREV + j
-            behind = rim_in[pl.ds(jnp.minimum(row + PREV, PREV), 1), :]
-            inside = bias[pl.ds(jnp.maximum(row, 0), 1), :]
-            earlier.append(jnp.where(row < 0, behind, inside) + switch(g, j))
+            source = rim_in if row < 0 else bias
+            earlier.append(source[pl.ds(row % PREV if row < 0 else row, 1), :] + switch(g, j))
         window(g, earlier, False)
 
     arrived(all_squares, square_send, square_recv, no - 1).wait_recv()
@@ -391,19 +475,31 @@
 
     @pl.when(owner)
     def _():
-        arrived(total, parts_send, parts_recv, owners - 1).wait_send()
-        arrived(prefixes, prefix_send, prefix_recv, ni - 1).wait_send()
-
-    @pl.when(jnp.logical_not(owner))
-    def _():
-        arrived(total, parts_send, parts_recv, owners).wait_send()
+        arrived(total, parts_send, parts_recv.at[0], owners - 1).wait_send()
+
+        @pl.when(first)
+        def _():
+            arrived(prefixes, prefix_send, prefix_recv, ni - 1).wait_send()
+
+        @pl.when(jnp.logical_not(first))
+        def _():
+            arrived(prefixes, prefix_send, prefix_recv, ni - 2).wait_send()
+
+    @pl.when(jnp.logical_not(jnp.logical_or(owner, last)))
+    def _():
+        arrived(total, parts_send, parts_recv.at[0], owners).wait_send()
 
     arrived(all_squares, square_send, square_recv, no - 1).wait_send()
 
     @pl.when(jnp.logical_not(last))
     def _():
-        for copy in rims:
-            copy.wait_send()
+        for n, (source, target, _) in enumerate(rims):
+            push(n, source, target, rim_send, rim_recv, following).wait_send()
+
+    @pl.when(relays)
+    def _():
+        for n, (_, target, relay) in enumerate(rims):
+            push(n, relay, target, hop_send, rim_recv, head).wait_send()
 
     for store in stores:
         store.wait()
@@ -448,14 +544,21 @@
             dma((2 * LOADS + 1,)),
             dma((groups,)),
             dma,
+            dma((ni // max(1, ni // 8),)),
             dma,
             dma,
-            dma,
-            dma((3,)),
-            dma((3,)),
+            dma((2 * PREV + 1,)),
+            dma((2 * PREV + 1,)),
             dma,
             dma,
             pltpu.SemaphoreType.REGULAR,
+            pltpu.SemaphoreType.REGULAR,
+            pltpu.SemaphoreType.REGULAR,
+            pltpu.VMEM((8, BLK), f32),
+            pltpu.VMEM((rim, wide), bf16),
+            pltpu.VMEM((rim, wide), bf16),
+            dma((2 * PREV + 1,)),
+            dma((2 * PREV + 1,)),
         ],
         compiler_params=pltpu.CompilerParams(
             collective_id=0, has_side_effects=True, vmem_limit_bytes=56 * 2**20

time: 38.7 us -> 33.3 us (0.86)
  the two profiles are of different devices: /device:TPU:1 before, /device:TPU:65 now
where the time goes in v3:
time: 33.3 us; the launch traced here: 32.9 us
  Pallas kernels  31 us (93%)
  local copies, waits for them, and re-layouts  1.87 us (6%)
    pallas_call x1, Pallas kernels, shards(): pl.pallas_call(functools.partial(kernel, ni, no, groups, heads), out_shap...  31 us
    unnamed x1, local copies, waits for them, and re-layouts  1.87 us

profile of v3, /device:TPU:65, one launch (start us, length us, event | category | flops | bytes accessed | tf_op | source)
XLA Modules:
  0.0 32.9 jit_solution(497423615421606890)
XLA Ops:
  0.0 31.0 %layer.1 = bf16[1024,256]{1,0:T(8,128)(2,1)} custom-call(s32[8]{0:T(128)} %counts_hbm.1, s32[3,8]{1,0:T(4,128)} %bitcast.2, f32[1,256]{1,0:T(1,128)} %bitcast.3, bf16[1024,256]{1,0:T(8,128)(2,1)} %q_hbm.1, bf16[1024,256]{1,0:T(8,128)(2,1)} %k_hbm.1, bf16[1024,256]{1,0:T(8,128)(2,1)} %v_hbm.1), custom_call_target="tpu_custom_call" | custom-call | tf_op jit(solution)/shard_map/layer/pallas_call | solution.py:517
  31.0 1.9 %copy.8 = bf16[1024,256]{1,0:T(8,128)(2,1)} copy(bf16[1024,256]{1,0:T(8,128)(2,1)} %layer.1) | data formatting | bytes 1048576

commit v4 on v3

--- a/solution.py
+++ b/solution.py
@@ -16,23 +16,8 @@
 LOG2E = 1.4426950408889634
 
 
-def torus(sizes):
-    def hops(step):
-        return sum(min(s, n - s) for s, n in zip(step, sizes))
-
-    steps = [()]
-    for n in sizes:
-        steps = [(*step, s) for step in steps for s in range(n)]
-    return sorted(steps[1:], key=hops, reverse=True)
-
-
-def moved(place, step, sizes):
-    index, stride = 0, 1
-    for s, n in zip(reversed(step), reversed(sizes)):
-        digit = lax.rem(place // stride, n) if stride > 1 else lax.rem(place, n)
-        index = index + lax.rem(digit + s, n) * stride
-        stride *= n
-    return index
+def far_first(size):
+    return sorted(range(size), key=lambda s: min(s, size - s), reverse=True)
 
 
 def dot_nt(a, b):
@@ -58,7 +43,7 @@
     q_hbm,
     k_hbm,
     v_hbm,
-    o_hbm,
+    out,
     counts_ref,
     mask_ref,
     gain_ref,
@@ -78,10 +63,8 @@
     squares,
     all_squares,
     scale,
-    out,
     small_sem,
     load_sem,
-    store_sem,
     parts_send,
     parts_recv,
     prefix_send,
@@ -127,10 +110,9 @@
 
     barrier = pltpu.get_barrier_semaphore()
     inner_sizes = {32: (4, 8), 8: (2, 4)}.get(ni, (1, ni))
-    outer_sizes = (8, 2) if no == 16 else (no,)
-    inner_peers = [{"inner": moved(here, step, inner_sizes)} for step in torus(inner_sizes)]
-    outer_peers = [{"outer": moved(stripe, step, outer_sizes)} for step in torus(outer_sizes)]
-    line = inner_sizes[-1]
+    outer_sizes = (8, 2) if no == 16 else (no, 1)
+    rows_of_chips, line = inner_sizes
+    layers, cores = outer_sizes
     half = line // 2
     owners = ni // 2
 
@@ -138,7 +120,7 @@
         return lax.rem(place, line) < half
 
     def rank(place):
-        return place // line * half + lax.rem(place, line)
+        return lax.div(place, line) * half + lax.rem(place, line)
 
     owner = owns(here)
     preceding = lax.rem(here + ni - 1, ni)
@@ -149,12 +131,40 @@
     relays = jnp.logical_and(tail, here >= line)
     ahead = lax.rem(here + line, ni)
     behind = lax.rem(here + ni - line, ni)
-    head = here // line * line
+    along, across = lax.rem(here, line), lax.div(here, line)
+    head = across * line
+    rows_far_first = [
+        (dx, lax.rem(across + dx, rows_of_chips) * line) for dx in far_first(rows_of_chips)
+    ]
+    tall, deep = lax.div(stripe, cores), lax.rem(stripe, cores)
+
+    def to_outer(act):
+        for dy in far_first(layers):
+            base = lax.rem(tall + dy, layers) * cores
+            for dc in range(cores):
+                if dy or dc:
+                    act({"outer": base + lax.rem(deep + dc, cores)})
+
+    def to_inner(act, only_owners):
+        for dz in far_first(line):
+            z = lax.rem(along + dz, line)
+
+            def send(dz=dz, z=z):
+                for dx, row in rows_far_first:
+                    if dx or dz:
+                        act(row + z, lax.div(row, 2) + z)
+
+            if only_owners:
+                pl.when(z < half)(send)
+            else:
+                send()
+
+    def greet(peer):
+        pl.semaphore_signal(barrier, inc=1, device_id=peer, device_id_type=MESH)
 
     @pl.when(owner)
     def _():
-        for peer in inner_peers:
-            pl.semaphore_signal(barrier, inc=1, device_id=peer, device_id_type=MESH)
+        to_inner(lambda there, _: greet({"inner": there}), False)
 
     @pl.when(jnp.logical_not(owner))
     def _():
@@ -168,8 +178,7 @@
 
     @pl.when(hub)
     def _():
-        for peer in outer_peers:
-            pl.semaphore_signal(barrier, inc=1, device_id=peer, device_id_type=MESH)
+        to_outer(greet)
 
     small[0].wait()
     lane = lax.broadcasted_iota(jnp.int32, (1, BLK), 1)
@@ -202,20 +211,14 @@
             device_id_type=MESH,
         )
 
-    for load in loads:
-        load.wait()
-
-    @pl.when(detour)
-    def _():
-        pl.semaphore_wait(barrier, greeters)
-        for n, (source, _, relay) in enumerate(rims):
-            push(n, source, relay, rim_send, hop_recv, ahead).start()
-
     token = lax.broadcasted_iota(jnp.int32, (BLK, HD), 0)
     each = owners // heads
     piece = heads * HD // owners
     running = [jnp.zeros((HD, HD), jnp.float32)] * heads
     for g in range(groups):
+        if (g * BLK) % chunk == 0:
+            loads[2 * (g * BLK // chunk)].wait()
+            loads[2 * (g * BLK // chunk) + 1].wait()
         for h in range(heads):
             cols = pl.ds(h * HD, HD)
             rows = pl.ds(rim + g * BLK, BLK)
@@ -227,31 +230,30 @@
         total[pl.ds(h * each, each)] = running[h].reshape(each, piece, HD).astype(jnp.bfloat16)
     within[0] = jnp.zeros(within.shape[1:], jnp.bfloat16)
 
-    @pl.when(jnp.logical_not(detour))
-    def _():
-        pl.semaphore_wait(barrier, greeters)
-
-    def send_part(peer):
-        there = peer["inner"]
-
-        @pl.when(owns(there))
-        def _():
-            pltpu.make_async_remote_copy(
-                src_ref=total.at[rank(there)],
-                dst_ref=parts.at[here],
-                send_sem=parts_send,
-                recv_sem=parts_recv.at[here // stage],
-                device_id=peer,
-                device_id_type=MESH,
-            ).start()
+    pl.semaphore_wait(barrier, greeters)
 
     stage = max(1, ni // 8)
     stages = ni // stage
+    my_stage = lax.div(here, stage)
+
+    def send_part(there, place):
+        pltpu.make_async_remote_copy(
+            src_ref=total.at[place],
+            dst_ref=parts.at[here],
+            send_sem=parts_send,
+            recv_sem=parts_recv.at[my_stage],
+            device_id={"inner": there},
+            device_id_type=MESH,
+        ).start()
 
     @pl.when(jnp.logical_not(last))
     def _():
-        for peer in inner_peers:
-            send_part(peer)
+        to_inner(send_part, True)
+
+    @pl.when(detour)
+    def _():
+        for n, (source, _, relay) in enumerate(rims):
+            push(n, source, relay, rim_send, hop_recv, ahead).start()
 
     @pl.when(straight)
     def _():
@@ -365,9 +367,10 @@
     def _():
         parts[pl.ds(here, 1)] = total[pl.ds(rank(here), 1)]
         so_far = jnp.zeros(parts.shape[1:], jnp.float32)
+        held = []
         for n in range(stages):
             members = stage - (n == stages - 1)
-            mine = here // stage == n
+            mine = my_stage == n
             for own in range(2):
                 if members > own:
 
@@ -379,13 +382,13 @@
             for m in following_spans:
                 so_far = so_far + parts[m - 1].astype(jnp.float32)
                 prefixes[m] = so_far.astype(jnp.bfloat16)
-            early = [m for m in following_spans if n == 0 and m % line < half]
-            for m in early:
-                send_prefix(m)
-            if n == 0:
+            for m in following_spans:
+                if m % line < half:
+                    send_prefix(m)
+            held += [m for m in following_spans if m % line >= half]
+            if n == stages - 1:
                 pl.semaphore_wait(ready, ni - owners)
-            for m in following_spans:
-                if m not in early:
+                for m in held:
                     send_prefix(m)
 
         @pl.when(jnp.logical_not(first))
@@ -395,8 +398,9 @@
     @pl.when(hub)
     def _():
         pl.semaphore_wait(entered, no - 1)
-        for peer in outer_peers:
-            pl.semaphore_signal(go, inc=1, device_id=peer, device_id_type=MESH)
+        to_outer(
+            lambda peer: pl.semaphore_signal(go, inc=1, device_id=peer, device_id_type=MESH)
+        )
 
     @pl.when(jnp.logical_and(owner, jnp.logical_not(first)))
     def _():
@@ -427,8 +431,8 @@
         pl.semaphore_wait(go, 1)
 
 
-    for peer in outer_peers:
-        pltpu.make_async_remote_copy(
+    to_outer(
+        lambda peer: pltpu.make_async_remote_copy(
             src_ref=squares,
             dst_ref=all_squares.at[stripe],
             send_sem=square_send,
@@ -436,7 +440,7 @@
             device_id=peer,
             device_id_type=MESH,
         ).start()
-
+    )
 
     def rim_here(n):
         source, target, _ = rims[n]
@@ -461,7 +465,6 @@
     scale[...] = lax.rsqrt(row_squares / width + 1e-6)
 
     small[2].wait()
-    stores = []
     for g in range(groups):
         rows = pl.ds(g * BLK, BLK)
         by_token = jnp.broadcast_to(scale[pl.ds(g, 1), :], (HD, BLK)).T
@@ -469,8 +472,6 @@
             cols = pl.ds(h * HD, HD)
             normed = lin[rows, cols] * by_token
             out[rows, cols] = (normed * gain_ref[:, cols] + local[rows, cols]).astype(jnp.bfloat16)
-        stores.append(pltpu.make_async_copy(out.at[rows], o_hbm.at[rows], store_sem.at[g]))
-        stores[-1].start()
 
 
     @pl.when(owner)
@@ -500,9 +501,6 @@
     def _():
         for n, (_, target, relay) in enumerate(rims):
             push(n, relay, target, hop_send, rim_recv, head).wait_send()
-
-    for store in stores:
-        store.wait()
 
 
 def shards(ni, no, queries, keys, values, counts, window_mask, norm_gain):
@@ -518,7 +516,7 @@
         functools.partial(kernel, ni, no, groups, heads),
         out_shape=jax.ShapeDtypeStruct((span, wide), bf16),
         in_specs=[any_space] * 6,
-        out_specs=any_space,
+        out_specs=pl.BlockSpec(memory_space=pltpu.VMEM),
         scratch_shapes=[
             pltpu.SMEM(counts.shape, jnp.int32),
             pltpu.SMEM(window_mask.shape[::-1], jnp.int32),
@@ -539,10 +537,8 @@
             pltpu.VMEM((groups, BLK), f32),
             pltpu.VMEM((no, groups, BLK), f32),
             pltpu.VMEM((groups, BLK), f32),
-            pltpu.VMEM((span, wide), bf16),
             dma((3,)),
             dma((2 * LOADS + 1,)),
-            dma((groups,)),
             dma,
             dma((ni // max(1, ni // 8),)),
             dma,
@@ -561,10 +557,10 @@
             dma((2 * PREV + 1,)),
         ],
         compiler_params=pltpu.CompilerParams(
-            collective_id=0, has_side_effects=True, vmem_limit_bytes=56 * 2**20
+            collective_id=0, has_side_effects=True, vmem_limit_bytes=40 * 2**20
         ),
         name="layer",
-    )(counts, window_mask.T, norm_gain.reshape(1, wide), queries, keys, values)
+    )(*(pltpu.with_memory_space_constraint(x, pltpu.HBM) for x in (counts, window_mask.T, norm_gain.reshape(1, wide), queries, keys, values)))
 
 
 def solution(mesh):

time: 33.3 us -> 31.5 us (0.946)
  local copies, waits for them, and re-layouts: 1.87 us -> 0.8 us
  Pallas kernels: 31 us -> 30.5 us
    unnamed x1, local copies, waits for them, and re-layouts: 1.87 us -> 0.8 us
    pallas_call x1, Pallas kernels: 31 us -> 30.5 us  [shards(): pl.pallas_call(functools.partial(kernel, ni, no, groups, heads), out_shap...]
where the time goes in v4:
time: 31.5 us; the launch traced here: 31.3 us
  Pallas kernels  30.5 us (97%)
  local copies, waits for them, and re-layouts  0.8 us (3%)
    pallas_call x1, Pallas kernels, shards(): pl.pallas_call(functools.partial(kernel, ni, no, groups, heads), out_shap...  30.5 us
    unnamed x1, local copies, waits for them, and re-layouts  0.8 us

profile of v4, /device:TPU:65, one launch (start us, length us, event | category | flops | bytes accessed | tf_op | source)
XLA Modules:
  0.0 31.3 jit_solution(5316508579340723384)
XLA Ops:
  0.0 30.5 %layer.1 = bf16[1024,256]{1,0:T(8,128)(2,1)S(1)} custom-call(s32[8]{0:T(128)} %counts_hbm.1, s32[3,8]{1,0:T(4,128)} %bitcast.2, f32[1,256]{1,0:T(1,128)} %bitcast.3, bf16[1024,256]{1,0:T(8,128)(2,1)} %q_hbm.1, bf16[1024,256]{1,0:T(8,128)(2,1)} %k_hbm.1, bf16[1024,256]{1,0:T(8,128)(2,1)} %v_hbm.1), custom_call_target="tpu_custom_call" | custom-call | tf_op jit(solution)/shard_map/layer/pallas_call | solution.py:515
  30.6 0.8 %copy.8 = bf16[1024,256]{1,0:T(8,128)(2,1)} copy(bf16[1024,256]{1,0:T(8,128)(2,1)S(1)} %layer.1) | data formatting | bytes 1048576

commit v5 on v4

--- a/solution.py
+++ b/solution.py
@@ -411,17 +411,26 @@
         arrived(before, prefix_send, prefix_recv, owners).wait_recv()
 
 
-    carried = [
-        before[pl.ds(h * each, each)].reshape(HD, HD) for h in range(heads)
-    ]
+    blank = jnp.zeros((HD, HD), jnp.bfloat16)
+    carried = jnp.concatenate(
+        [
+            jnp.concatenate(
+                [
+                    before[pl.ds(h * each, each)].reshape(HD, HD) if h == n else blank
+                    for n in range(heads)
+                ],
+                axis=1,
+            )
+            for h in range(heads)
+        ],
+        axis=0,
+    )
     for g in range(groups):
         rows = pl.ds(g * BLK, BLK)
-        powers = jnp.zeros((BLK, HD), jnp.float32)
-        for h in range(heads):
-            cols = pl.ds(h * HD, HD)
-            whole = lin[rows, cols] + dot_nn(q_all[rows, cols], carried[h])
-            lin[rows, cols] = whole
-            powers = powers + whole * whole
+        whole = lin[rows, :] + dot_nn(q_all[rows, :], carried)
+        lin[rows, :] = whole
+        powers = whole * whole
+        powers = sum(powers[:, h * HD : (h + 1) * HD] for h in range(heads))
         squares[pl.ds(g, 1), :] = jnp.sum(powers.T, axis=0, keepdims=True)
 
     all_squares[pl.ds(stripe, 1)] = squares[...][None]

time: 31.5 us -> 31.5 us (level)
  no operation moved by 1% of the time
where the time goes in v5:
time: 31.5 us; the launch traced here: 31.3 us
  Pallas kernels  30.5 us (97%)
  local copies, waits for them, and re-layouts  0.8 us (3%)
    pallas_call x1, Pallas kernels, shards(): pl.pallas_call(functools.partial(kernel, ni, no, groups, heads), out_shap...  30.5 us
    unnamed x1, local copies, waits for them, and re-layouts  0.8 us

profile of v5, /device:TPU:65, one launch (start us, length us, event | category | flops | bytes accessed | tf_op | source)
XLA Modules:
  0.0 31.3 jit_solution(9850133926179267660)
XLA Ops:
  0.0 30.5 %layer.1 = bf16[1024,256]{1,0:T(8,128)(2,1)S(1)} custom-call(s32[8]{0:T(128)} %counts_hbm.1, s32[3,8]{1,0:T(4,128)} %bitcast.2, f32[1,256]{1,0:T(1,128)} %bitcast.3, bf16[1024,256]{1,0:T(8,128)(2,1)} %q_hbm.1, bf16[1024,256]{1,0:T(8,128)(2,1)} %k_hbm.1, bf16[1024,256]{1,0:T(8,128)(2,1)} %v_hbm.1), custom_call_target="tpu_custom_call" | custom-call | tf_op jit(solution)/shard_map/layer/pallas_call | solution.py:524
  30.6 0.8 %copy.8 = bf16[1024,256]{1,0:T(8,128)(2,1)} copy(bf16[1024,256]{1,0:T(8,128)(2,1)S(1)} %layer.1) | data formatting | bytes 1048576

commit v6 on v5

--- a/solution.py
+++ b/solution.py
@@ -10,7 +10,7 @@
 HD = 128
 BLK = 128
 PREV = 3
-LOADS = 4
+LOADS = 2
 MESH = pl.DeviceIdType.MESH
 NEG = -1e30
 LOG2E = 1.4426950408889634

time: 31.5 us -> 31.4 us (level)
  no operation moved by 1% of the time
where the time goes in v6:
time: 31.4 us; the launch traced here: 31.3 us
  Pallas kernels  30.5 us (97%)
  local copies, waits for them, and re-layouts  0.8 us (3%)
    pallas_call x1, Pallas kernels, shards(): pl.pallas_call(functools.partial(kernel, ni, no, groups, heads), out_shap...  30.5 us
    unnamed x1, local copies, waits for them, and re-layouts  0.8 us

profile of v6, /device:TPU:65, one launch (start us, length us, event | category | flops | bytes accessed | tf_op | source)
XLA Modules:
  0.0 31.3 jit_solution(15952845662596880475)
XLA Ops:
  0.0 30.5 %layer.1 = bf16[1024,256]{1,0:T(8,128)(2,1)S(1)} custom-call(s32[8]{0:T(128)} %counts_hbm.1, s32[3,8]{1,0:T(4,128)} %bitcast.2, f32[1,256]{1,0:T(1,128)} %bitcast.3, bf16[1024,256]{1,0:T(8,128)(2,1)} %q_hbm.1, bf16[1024,256]{1,0:T(8,128)(2,1)} %k_hbm.1, bf16[1024,256]{1,0:T(8,128)(2,1)} %v_hbm.1), custom_call_target="tpu_custom_call" | custom-call | tf_op jit(solution)/shard_map/layer/pallas_call | solution.py:524
  30.5 0.8 %copy.8 = bf16[1024,256]{1,0:T(8,128)(2,1)} copy(bf16[1024,256]{1,0:T(8,128)(2,1)S(1)} %layer.1) | data formatting | bytes 1048576
